TPU v7x, 32 devices: a whole 2x2x4 slice. The times are simulated.
32 devices in a mesh: pix: 16 (over z, x, core), rep: 2 (over y).
Axes of the slice: x: 2, y: 2, z: 4, core: 2. Of those that a mesh axis runs over, the one named last changes fastest.
Arguments:
- tokens: bfloat16 [256, 16, 1152], P(('pix', 'rep')), may hold values from -48 to 48
- out_grad: bfloat16 [256, 16, 1152], P(('pix', 'rep')), may hold values from -6 to 6
- query_weight: bfloat16 [1152, 1152], P('pix'), may hold values from -0.1875 to 0.1875
- key_weight: bfloat16 [1152, 1152], P('pix'), may hold values from -0.1875 to 0.1875
- value_weight: bfloat16 [1152, 1152], P('pix'), may hold values from -0.1875 to 0.1875
- output_weight: bfloat16 [1152, 1152], P('pix'), may hold values from -0.1875 to 0.1875
Outputs:
- input_grad: bfloat16 [256, 16, 1152], P(('pix', 'rep'))
- weight_grads: float32 [1152, 4608], P('pix')
All inputs are finite; a program needn't handle non-finite values.
Results may differ from a plain program's by a relative error of at most 0.025.
The roundings to bfloat16 on the way count: a program that leaves them out, or rounds other values in their place, can miss the bound.
Values may be sent and summed in bfloat16 or wider, within the bound.
No kernel may reach another device: no remote copies, remote signals or barrier semaphores. Data moves between devices by JAX's collectives and lax.ppermute only.
A program may use at most 128 MiB of HBM per device.

v0:
```python
import jax
import jax.numpy as jnp
from jax import lax
from jax.sharding import PartitionSpec as P

D = 1152
HEADS = 16
HEAD_DIM = 72
FRAMES = 16


def contract_last(left, right):
    return lax.dot_general(
        left, right, (((1,), (1,)), ((), ())), preferred_element_type=jnp.float32
    )


def contract_first(left, right):
    return lax.dot_general(
        left, right, (((0,), (0,)), ((), ())), preferred_element_type=jnp.float32
    )


def local(tokens, out_grad, query_weight, key_weight, value_weight, output_weight):
    count = tokens.shape[0]
    rows = tokens.reshape(-1, D)
    drows = out_grad.reshape(-1, D)
    scale = 1.0 / HEAD_DIM**0.5
    full_q, full_k, full_v = (
        lax.all_gather(query_weight, "pix", axis=0, tiled=True),
        lax.all_gather(key_weight, "pix", axis=0, tiled=True),
        lax.all_gather(value_weight, "pix", axis=0, tiled=True),
    )
    query = jnp.dot(rows, full_q, preferred_element_type=jnp.float32).astype(jnp.bfloat16)
    keyed = jnp.dot(rows, full_k, preferred_element_type=jnp.float32).astype(jnp.bfloat16)
    valued = jnp.dot(rows, full_v, preferred_element_type=jnp.float32).astype(jnp.bfloat16)
    shape4 = (count, FRAMES, HEADS, HEAD_DIM)
    qh = query.reshape(shape4)
    kh = keyed.reshape(shape4)
    vh = valued.reshape(shape4)
    scores = jnp.einsum("sfhe,sghe->shfg", qh, kh, preferred_element_type=jnp.float32) * scale
    scores = scores - jnp.max(scores, axis=-1, keepdims=True)
    expo = jnp.exp(scores)
    probs = expo / jnp.sum(expo, axis=-1, keepdims=True)
    probs_b = probs.astype(jnp.bfloat16)
    attended = (
        jnp.einsum("shfg,sghe->sfhe", probs_b, vh, preferred_element_type=jnp.float32)
        .reshape(-1, D)
        .astype(jnp.bfloat16)
    )
    output_full = lax.all_gather(output_weight, "pix", axis=0, tiled=True)
    dattn = contract_last(drows, output_full).astype(jnp.bfloat16)
    dah = dattn.reshape(shape4)
    dvalue = (
        jnp.einsum("shfg,sfhe->sghe", probs_b, dah, preferred_element_type=jnp.float32)
        .reshape(-1, D)
        .astype(jnp.bfloat16)
    )
    dprobs = jnp.einsum("sfhe,sghe->shfg", dah, vh, preferred_element_type=jnp.float32)
    dscore = (probs * (dprobs - jnp.sum(dprobs * probs, axis=-1, keepdims=True)) * scale).astype(
        jnp.bfloat16
    )
    dquery = (
        jnp.einsum("shfg,sghe->sfhe", dscore, kh, preferred_element_type=jnp.float32)
        .reshape(-1, D)
        .astype(jnp.bfloat16)
    )
    dkey = (
        jnp.einsum("shfg,sfhe->sghe", dscore, qh, preferred_element_type=jnp.float32)
        .reshape(-1, D)
        .astype(jnp.bfloat16)
    )
    grads = lax.psum_scatter(
        jnp.concatenate(
            [
                jnp.concatenate(
                    [
                        contract_first(rows, dquery),
                        contract_first(rows, dkey),
                        contract_first(rows, dvalue),
                    ],
                    axis=1,
                ),
                contract_first(attended, drows),
            ],
            axis=1,
        ).astype(jnp.bfloat16),
        "pix",
        scatter_dimension=0,
        tiled=True,
    ).astype(jnp.float32)
    back_q, back_k, back_v = (
        lax.all_gather(query_weight, "pix", axis=0, tiled=True),
        lax.all_gather(key_weight, "pix", axis=0, tiled=True),
        lax.all_gather(value_weight, "pix", axis=0, tiled=True),
    )
    dinput = (
        contract_last(dquery, back_q) + contract_last(dkey, back_k) + contract_last(dvalue, back_v)
    )
    weight_grads = lax.psum(grads, "rep")
    return (dinput.astype(jnp.bfloat16).reshape(tokens.shape), weight_grads)


def solution(mesh):
    placed = (
        P(("pix", "rep"), None, None),
        P(("pix", "rep"), None, None),
        P("pix", None),
        P("pix", None),
        P("pix", None),
        P("pix", None),
    )
    return jax.shard_map(
        local,
        mesh=mesh,
        in_specs=placed,
        out_specs=(P(("pix", "rep"), None, None), P("pix", None)),
        check_vma=False,
    )
```

profile of v0, /device:TPU:0, one launch (start us, length us, event | category | flops | bytes accessed | tf_op | source)
XLA Modules:
  0.0 441.2 jit_solution(11428805849281007432)
XLA Ops:
  10.0 46.1 %all-gather.9.cloned.1.call-done = bf16[1152,1152]{1,0:T(8,128)(2,1)} async-done(((bf16[72,1152]{1,0:T(8,128)(2,1)}), bf16[1152,1152]{1,0:T(8,128)(2,1)}) %all-gather.9.cloned.1.call-update) | async-done | bytes 2654224 | tf_op jit(solution)/shard_map/all_gather | solution.py:51
  56.1 2.8 convolution_convert_fusion.5
  59.8 40.5 %all-gather.11.cloned.1.call-done = bf16[1152,1152]{1,0:T(8,128)(2,1)} async-done(((bf16[72,1152]{1,0:T(8,128)(2,1)}), bf16[1152,1152]{1,0:T(8,128)(2,1)}) %all-gather.11.cloned.1.call-update) | async-done | bytes 2654224 | tf_op jit(solution)/shard_map/all_gather | solution.py:32
  100.3 2.3 convolution_convert_fusion.4
  102.6 0.9 reshape.44
  103.6 40.9 %all-gather.5.cloned.1.call-done = bf16[1152,1152]{1,0:T(8,128)(2,1)} async-done(((bf16[72,1152]{1,0:T(8,128)(2,1)}), bf16[1152,1152]{1,0:T(8,128)(2,1)}) %all-gather.5.cloned.1.call-update) | async-done | bytes 2654224 | tf_op jit(solution)/shard_map/all_gather | solution.py:31
  144.5 2.3 convolution_convert_fusion.7
  147.8 40.8 %all-gather.7.cloned.1.call-done = bf16[1152,1152]{1,0:T(8,128)(2,1)} async-done(((bf16[72,1152]{1,0:T(8,128)(2,1)}), bf16[1152,1152]{1,0:T(8,128)(2,1)}) %all-gather.7.cloned.1.call-update) | async-done | bytes 2654224 | tf_op jit(solution)/shard_map/all_gather | solution.py:30
  188.6 2.3 convolution_convert_fusion.6
  190.9 0.9 reshape.41
  192.3 1.7 fusion.48
  194.0 2.3 fusion.14
  196.3 2.3 fusion.13
  198.6 3.0 fusion.12
  201.6 1.6 fusion.15
  209.7 28.0 %pad_maximum_fusion = bf16[1152,4608]{0,1:T(8,128)(2,1)} fusion(bf16[1152,1152]{0,1:T(8,128)(2,1)S(1)} %convolution_convert_fusion, bf16[1152,1152]{0,1:T(8,128)(2,1)S(1)} %fusion.4, bf16[1152,1152]{0,1:T(8,128)(2,1)S(1)} %fusion.3, bf16[1152,1152]{0,1:T(8,128)(2,1)S(1)} %fusion.2), kind=kLoop, calls=%fused_computation.2 | loop fusion | flops 42467328 | bytes 21233664 | tf_op jit(solution)/shard_map/concatenate | solution.py:74
  237.7 15.3 %copy.51 = bf16[1152,4608]{1,0:T(8,128)(2,1)} copy(bf16[1152,4608]{0,1:T(8,128)(2,1)} %pad_maximum_fusion) | data formatting | bytes 21233664
  253.0 1.7 copy-done.2
  257.4 1.2 copy-done.3
  258.7 1.6 fusion.5
  260.3 112.4 %reduce-scatter.4.cloned.1.call-done = bf16[72,4608]{1,0:T(8,128)(2,1)} async-done(((bf16[1152,4608]{1,0:T(8,128)(2,1)}), bf16[72,4608]{1,0:T(8,128)(2,1)}) %reduce-scatter.4.cloned.1.call-update) | async-done | bytes 663568
  372.7 2.3 copy.52
  375.0 57.9 %all-reduce.1 = f32[72,4608]{0,1:T(8,128)S(1)} all-reduce(bf16[72,4608]{0,1:T(8,128)(2,1)} %copy.52), channel_id=1, replica_groups=mesh['pix'=16,'rep'=2] {'rep'}, use_global_device_ids=true, to_apply=%region_4.0 | all-reduce | flops 331776 | bytes 1990656 | tf_op jit(solution)/shard_map/psum | solution.py:100
  432.9 1.7 copy.48
  (45 shorter events, 13.9 us)
Async XLA Ops:
  7.2 93.1 %copy-start = (bf16[8,16,1152]{2,1,0:T(8,128)(2,1)S(1)}, bf16[8,16,1152]{2,1,0:T(8,128)(2,1)}, u32[]{:S(2)}) copy-start(bf16[8,16,1152]{2,1,0:T(8,128)(2,1)} %param.6) | copy-start | bytes 884740
  7.2 48.9 %all-gather.9.cloned.1.call-start = ((), (), s32[]{:S(2)}) async-start(), calls=%async_computation.3 | async-start | bytes 2820096 | tf_op jit(solution)/shard_map/all_gather | solution.py:51
  7.9 92.4 %all-gather.11.cloned.1.call-start = ((), (), s32[]{:S(2)}) async-start(), calls=%async_computation.4 | async-start | bytes 2820096 | tf_op jit(solution)/shard_map/all_gather | solution.py:32
  8.7 135.8 %all-gather.5.cloned.1.call-start = ((), (), s32[]{:S(2)}) async-start(), calls=%async_computation.1 | async-start | bytes 2820096 | tf_op jit(solution)/shard_map/all_gather | solution.py:31
  9.4 179.2 %all-gather.7.cloned.1.call-start = ((), (), s32[]{:S(2)}) async-start(), calls=%async_computation.2 | async-start | bytes 2820096 | tf_op jit(solution)/shard_map/all_gather | solution.py:30
  10.0 362.7 %reduce-scatter.4.cloned.1.call-start = ((), (), s32[]{:S(2)}) async-start(), calls=%async_computation.5 | async-start | bytes 11280384
  191.9 2.1 copy-start.9
  201.6 1.7 copy-start.8
  203.3 1.3 copy-start.7
  203.9 2.0 copy-start.4
  206.8 1.8 copy-start.6
  253.0 1.7 copy-start.2
  254.7 1.7 copy-start.1
  256.5 2.2 copy-start.3
  256.5 2.2 copy-start.5
Sparse Core Ops, SparseCore 0:
  10.1 45.8 all-gather.8
  58.2 42.0 all-gather.10
  102.4 42.0 all-gather.4
  146.5 42.0 all-gather.6
  253.1 119.5 reduce-scatter.3
where the time goes:
time: 442 us; the launch traced here: 441 us
  waiting for transfers between devices  283 us (64%)
  blocking collectives  57.9 us (13%)
  local copies, waits for them, and re-layouts  29.5 us (7%)
  matrix products  28.1 us (6%)
  other arithmetic  28 us (6%)
  between operations  14.2 us (3%)
    unnamed x6, waiting for transfers between devices  115 us
    psum x1, blocking collectives, local(): weight_grads = lax.psum(grads, 'rep')  57.9 us
    all_gather x1, waiting for transfers between devices, local(): output_full = lax.all_gather(output_weight, 'pix', axis=0, tiled=True)  46.1 us
    all_gather x1, waiting for transfers between devices, local(): lax.all_gather(key_weight, 'pix', axis=0, tiled=True)  40.9 us
    all_gather x1, waiting for transfers between devices, local(): lax.all_gather(query_weight, 'pix', axis=0, tiled=True)  40.8 us
    all_gather x1, waiting for transfers between devices, local(): lax.all_gather(value_weight, 'pix', axis=0, tiled=True)  40.5 us
    concatenate x1, other arithmetic, local(): jnp.concatenate([jnp.concatenate([contract_first(rows, dquery), contract_...  28 us
    unnamed x23, local copies, waits for them, and re-layouts  23.2 us
  transfers between devices with their start and end apart: 5, of which 5 were waited for; matrix products, arithmetic and copies ran while one was open for 3% of the time, Pallas kernels for 0%

commit v1 on v0

--- a/solution.py
+++ b/solution.py
@@ -48,7 +48,12 @@
         .reshape(-1, D)
         .astype(jnp.bfloat16)
     )
-    output_full = lax.all_gather(output_weight, "pix", axis=0, tiled=True)
+    ring = [output_weight]
+    for hop in range(15):
+        ring.append(lax.ppermute(ring[-1], "pix", [(dev, (dev + 1) % 16) for dev in range(16)]))
+    output_full = jnp.roll(
+        jnp.concatenate(ring[::-1], axis=0), (lax.axis_index("pix") + 1) * ring[0].shape[0], axis=0
+    )
     dattn = contract_last(drows, output_full).astype(jnp.bfloat16)
     dah = dattn.reshape(shape4)
     dvalue = (

time: 442 us -> 426 us (0.964)
  waiting for transfers between devices: 283 us -> 264 us
    ppermute x0 -> x15, waiting for transfers between devices: none -> 121 us  [local(): lax.ppermute(ring[-1], 'pix', [(dev, (dev + 1) % 16) for dev in range(16)])]
    all_gather x1 -> x0, waiting for transfers between devices: 46.1 us -> none  [local(): output_full = lax.all_gather(output_weight, 'pix', axis=0, tiled=True)]
    all_gather x1, waiting for transfers between devices: 40.9 us -> 0.02 us  [local(): lax.all_gather(key_weight, 'pix', axis=0, tiled=True)]
    all_gather x1, waiting for transfers between devices: 40.5 us -> 0.02 us  [local(): lax.all_gather(value_weight, 'pix', axis=0, tiled=True)]
    all_gather x1, waiting for transfers between devices: 40.8 us -> 27.5 us  [local(): lax.all_gather(query_weight, 'pix', axis=0, tiled=True)]
    unnamed x23 -> x50, local copies, waits for them, and re-layouts: 23.2 us -> 20 us
    unnamed x6 -> x5, waiting for transfers between devices: 115 us -> 116 us
  transfers between devices with their start and end apart: 5 -> 19, of which waited for: 5 -> 17; matrix products, arithmetic and copies ran while one was open for 3% -> 3% of each run, Pallas kernels for 0% -> 0%
where the time goes in v1:
time: 426 us; the launch traced here: 425 us
  waiting for transfers between devices  264 us (62%)
  blocking collectives  57.9 us (14%)
  matrix products  30.2 us (7%)
  local copies, waits for them, and re-layouts  29.5 us (7%)
  other arithmetic  28 us (7%)
  between operations  14.3 us (3%)
    ppermute x15, waiting for transfers between devices, local(): lax.ppermute(ring[-1], 'pix', [(dev, (dev + 1) % 16) for dev in range(16)])  121 us
    unnamed x5, waiting for transfers between devices  116 us
    psum x1, blocking collectives, local(): weight_grads = lax.psum(grads, 'rep')  57.9 us
    concatenate x1, other arithmetic, local(): jnp.concatenate([jnp.concatenate([contract_first(rows, dquery), contract_...  28 us
    all_gather x1, waiting for transfers between devices, local(): lax.all_gather(query_weight, 'pix', axis=0, tiled=True)  27.5 us
    unnamed x50, local copies, waits for them, and re-layouts  20 us
  transfers between devices with their start and end apart: 19, of which 17 were waited for; matrix products, arithmetic and copies ran while one was open for 3% of the time, Pallas kernels for 0%

profile of v1, /device:TPU:0, one launch (start us, length us, event | category | flops | bytes accessed | tf_op | source)
XLA Modules:
  0.0 424.7 jit_solution(16417071076089501022)
XLA Ops:
  9.3 8.2 %collective-permute-done = bf16[72,1152]{1,0:T(8,128)(2,1)S(1)} collective-permute-done((bf16[72,1152]{1,0:T(8,128)(2,1)}, bf16[72,1152]{1,0:T(8,128)(2,1)S(1)}, u32[]{:S(2)}, u32[]{:S(2)}) %collective-permute-start) | collective-permute-done | bytes 165920 | tf_op jit(solution)/shard_map/ppermute | solution.py:53
  17.5 7.6 %collective-permute-done.1 = bf16[72,1152]{1,0:T(8,128)(2,1)S(1)} collective-permute-done((bf16[72,1152]{1,0:T(8,128)(2,1)S(1)}, bf16[72,1152]{1,0:T(8,128)(2,1)S(1)}, u32[]{:S(2)}, u32[]{:S(2)}) %collective-permute-start.1) | collective-permute-done | bytes 165920 | tf_op jit(solution)/shard_map/ppermute | solution.py:53
  25.0 8.8 %collective-permute-done.2 = bf16[72,1152]{1,0:T(8,128)(2,1)S(1)} collective-permute-done((bf16[72,1152]{1,0:T(8,128)(2,1)S(1)}, bf16[72,1152]{1,0:T(8,128)(2,1)S(1)}, u32[]{:S(2)}, u32[]{:S(2)}) %collective-permute-start.2) | collective-permute-done | bytes 165920 | tf_op jit(solution)/shard_map/ppermute | solution.py:53
  33.8 7.5 %collective-permute-done.3 = bf16[72,1152]{1,0:T(8,128)(2,1)S(1)} collective-permute-done((bf16[72,1152]{1,0:T(8,128)(2,1)S(1)}, bf16[72,1152]{1,0:T(8,128)(2,1)S(1)}, u32[]{:S(2)}, u32[]{:S(2)}) %collective-permute-start.3) | collective-permute-done | bytes 165920 | tf_op jit(solution)/shard_map/ppermute | solution.py:53
  41.3 10.0 %collective-permute-done.4 = bf16[72,1152]{1,0:T(8,128)(2,1)S(1)} collective-permute-done((bf16[72,1152]{1,0:T(8,128)(2,1)S(1)}, bf16[72,1152]{1,0:T(8,128)(2,1)S(1)}, u32[]{:S(2)}, u32[]{:S(2)}) %collective-permute-start.4) | collective-permute-done | bytes 165920 | tf_op jit(solution)/shard_map/ppermute | solution.py:53
  51.3 8.2 %collective-permute-done.5 = bf16[72,1152]{1,0:T(8,128)(2,1)S(1)} collective-permute-done((bf16[72,1152]{1,0:T(8,128)(2,1)S(1)}, bf16[72,1152]{1,0:T(8,128)(2,1)S(1)}, u32[]{:S(2)}, u32[]{:S(2)}) %collective-permute-start.5) | collective-permute-done | bytes 165920 | tf_op jit(solution)/shard_map/ppermute | solution.py:53
  59.5 7.5 %collective-permute-done.6 = bf16[72,1152]{1,0:T(8,128)(2,1)S(1)} collective-permute-done((bf16[72,1152]{1,0:T(8,128)(2,1)S(1)}, bf16[72,1152]{1,0:T(8,128)(2,1)S(1)}, u32[]{:S(2)}, u32[]{:S(2)}) %collective-permute-start.6) | collective-permute-done | bytes 165920 | tf_op jit(solution)/shard_map/ppermute | solution.py:53
  66.9 9.1 %collective-permute-done.7 = bf16[72,1152]{1,0:T(8,128)(2,1)S(1)} collective-permute-done((bf16[72,1152]{1,0:T(8,128)(2,1)S(1)}, bf16[72,1152]{1,0:T(8,128)(2,1)S(1)}, u32[]{:S(2)}, u32[]{:S(2)}) %collective-permute-start.7) | collective-permute-done | bytes 165920 | tf_op jit(solution)/shard_map/ppermute | solution.py:53
  76.0 7.8 %collective-permute-done.8 = bf16[72,1152]{1,0:T(8,128)(2,1)S(1)} collective-permute-done((bf16[72,1152]{1,0:T(8,128)(2,1)S(1)}, bf16[72,1152]{1,0:T(8,128)(2,1)S(1)}, u32[]{:S(2)}, u32[]{:S(2)}) %collective-permute-start.8) | collective-permute-done | bytes 165920 | tf_op jit(solution)/shard_map/ppermute | solution.py:53
  83.8 7.6 %collective-permute-done.9 = bf16[72,1152]{1,0:T(8,128)(2,1)S(1)} collective-permute-done((bf16[72,1152]{1,0:T(8,128)(2,1)S(1)}, bf16[72,1152]{1,0:T(8,128)(2,1)S(1)}, u32[]{:S(2)}, u32[]{:S(2)}) %collective-permute-start.9) | collective-permute-done | bytes 165920 | tf_op jit(solution)/shard_map/ppermute | solution.py:53
  91.4 8.7 %collective-permute-done.10 = bf16[72,1152]{1,0:T(8,128)(2,1)S(1)} collective-permute-done((bf16[72,1152]{1,0:T(8,128)(2,1)S(1)}, bf16[72,1152]{1,0:T(8,128)(2,1)S(1)}, u32[]{:S(2)}, u32[]{:S(2)}) %collective-permute-start.10) | collective-permute-done | bytes 165920 | tf_op jit(solution)/shard_map/ppermute | solution.py:53
  100.1 7.7 %collective-permute-done.11 = bf16[72,1152]{1,0:T(8,128)(2,1)S(1)} collective-permute-done((bf16[72,1152]{1,0:T(8,128)(2,1)S(1)}, bf16[72,1152]{1,0:T(8,128)(2,1)S(1)}, u32[]{:S(2)}, u32[]{:S(2)}) %collective-permute-start.11) | collective-permute-done | bytes 165920 | tf_op jit(solution)/shard_map/ppermute | solution.py:53
  107.9 7.5 %collective-permute-done.12 = bf16[72,1152]{1,0:T(8,128)(2,1)S(1)} collective-permute-done((bf16[72,1152]{1,0:T(8,128)(2,1)S(1)}, bf16[72,1152]{1,0:T(8,128)(2,1)S(1)}, u32[]{:S(2)}, u32[]{:S(2)}) %collective-permute-start.12) | collective-permute-done | bytes 165920 | tf_op jit(solution)/shard_map/ppermute | solution.py:53
  115.3 7.5 %collective-permute-done.13 = bf16[72,1152]{1,0:T(8,128)(2,1)S(1)} collective-permute-done((bf16[72,1152]{1,0:T(8,128)(2,1)S(1)}, bf16[72,1152]{1,0:T(8,128)(2,1)S(1)}, u32[]{:S(2)}, u32[]{:S(2)}) %collective-permute-start.13) | collective-permute-done | bytes 165920 | tf_op jit(solution)/shard_map/ppermute | solution.py:53
  122.9 7.3 %collective-permute-done.14 = bf16[72,1152]{1,0:T(8,128)(2,1)S(1)} collective-permute-done((bf16[72,1152]{1,0:T(8,128)(2,1)S(1)}, bf16[72,1152]{1,0:T(8,128)(2,1)S(1)}, u32[]{:S(2)}, u32[]{:S(2)}) %collective-permute-start.14) | collective-permute-done | bytes 165920 | tf_op jit(solution)/shard_map/ppermute | solution.py:53
  139.9 27.5 %all-gather.6.cloned.1.call-done = bf16[1152,1152]{1,0:T(8,128)(2,1)} async-done(((bf16[72,1152]{1,0:T(8,128)(2,1)}), bf16[1152,1152]{1,0:T(8,128)(2,1)}) %all-gather.6.cloned.1.call-update) | async-done | bytes 2654224 | tf_op jit(solution)/shard_map/all_gather | solution.py:30
  171.8 2.7 fusion.57
  174.6 3.0 fusion.20
  177.6 3.1 fusion.21
  193.1 28.0 %pad_maximum_fusion = bf16[1152,4608]{0,1:T(8,128)(2,1)} fusion(bf16[1152,1152]{0,1:T(8,128)(2,1)S(1)} %convolution_convert_fusion, bf16[1152,1152]{0,1:T(8,128)(2,1)S(1)} %fusion.4, bf16[1152,1152]{0,1:T(8,128)(2,1)S(1)} %fusion.3, bf16[1152,1152]{0,1:T(8,128)(2,1)S(1)} %fusion.2), kind=kLoop, calls=%fused_computation.2 | loop fusion | flops 42467328 | bytes 21233664 | tf_op jit(solution)/shard_map/concatenate | solution.py:79
  221.1 15.3 %copy.53 = bf16[1152,4608]{1,0:T(8,128)(2,1)} copy(bf16[1152,4608]{0,1:T(8,128)(2,1)} %pad_maximum_fusion) | data formatting | bytes 21233664
  236.5 2.8 fusion.62
  241.9 114.3 %reduce-scatter.4.cloned.1.call-done = bf16[72,4608]{1,0:T(8,128)(2,1)} async-done(((bf16[1152,4608]{1,0:T(8,128)(2,1)}), bf16[72,4608]{1,0:T(8,128)(2,1)}) %reduce-scatter.4.cloned.1.call-update) | async-done | bytes 663568
  358.5 57.9 %all-reduce.1 = f32[72,4608]{0,1:T(8,128)S(1)} all-reduce(bf16[72,4608]{0,1:T(8,128)(2,1)} %copy.54), channel_id=1, replica_groups=mesh['pix'=16,'rep'=2] {'rep'}, use_global_device_ids=true, to_apply=%region_4.5 | all-reduce | flops 331776 | bytes 1990656 | tf_op jit(solution)/shard_map/psum | solution.py:105
  (101 shorter events, 35.0 us)
Async XLA Ops:
  7.2 126.1 %copy-start = (bf16[8,16,1152]{2,1,0:T(8,128)(2,1)S(1)}, bf16[8,16,1152]{2,1,0:T(8,128)(2,1)}, u32[]{:S(2)}) copy-start(bf16[8,16,1152]{2,1,0:T(8,128)(2,1)} %param.6) | copy-start | bytes 884740
  7.2 123.5 %copy-start.6 = (bf16[72,1152]{1,0:T(8,128)(2,1)S(1)}, bf16[72,1152]{1,0:T(8,128)(2,1)}, u32[]{:S(2)}) copy-start(bf16[72,1152]{1,0:T(8,128)(2,1)} %param.11) | copy-start | bytes 497668
  7.2 126.0 %all-gather.8.cloned.1.call-start = ((), (), s32[]{:S(2)}) async-start(), calls=%async_computation.3 | async-start | bytes 2820096 | tf_op jit(solution)/shard_map/all_gather | solution.py:32
  7.9 128.6 %all-gather.4.cloned.1.call-start = ((), (), s32[]{:S(2)}) async-start(), calls=%async_computation.1 | async-start | bytes 2820096 | tf_op jit(solution)/shard_map/all_gather | solution.py:31
  8.7 158.6 %all-gather.6.cloned.1.call-start = ((), (), s32[]{:S(2)}) async-start(), calls=%async_computation.2 | async-start | bytes 2820096 | tf_op jit(solution)/shard_map/all_gather | solution.py:30
  8.7 8.7 %collective-permute-start = (bf16[72,1152]{1,0:T(8,128)(2,1)}, bf16[72,1152]{1,0:T(8,128)(2,1)S(1)}, u32[]{:S(2)}, u32[]{:S(2)}) collective-permute-start(bf16[72,1152]{1,0:T(8,128)(2,1)} %param.11), channel_id=1, source_target_pairs={{0,2},{2,4},{4,6},{6,8},{8,10},{10,12},{12,14},{14,16},{16,18},{18... | collective-permute-start | bytes 497672 | tf_op jit(solution)/shard_map/ppermute | solution.py:53
  17.5 7.6 %collective-permute-start.1 = (bf16[72,1152]{1,0:T(8,128)(2,1)S(1)}, bf16[72,1152]{1,0:T(8,128)(2,1)S(1)}, u32[]{:S(2)}, u32[]{:S(2)}) collective-permute-start(bf16[72,1152]{1,0:T(8,128)(2,1)S(1)} %collective-permute-done), channel_id=1, source_target_pairs={{0,2},{2,4},{4,6},{6,8},{8,10},{10,12},{12,14},{14,16},{16,18},{18... | collective-permute-start | bytes 497672 | tf_op jit(solution)/shard_map/ppermute | solution.py:53
  25.0 8.8 %collective-permute-start.2 = (bf16[72,1152]{1,0:T(8,128)(2,1)S(1)}, bf16[72,1152]{1,0:T(8,128)(2,1)S(1)}, u32[]{:S(2)}, u32[]{:S(2)}) collective-permute-start(bf16[72,1152]{1,0:T(8,128)(2,1)S(1)} %collective-permute-done.1), channel_id=1, source_target_pairs={{0,2},{2,4},{4,6},{6,8},{8,10},{10,12},{12,14},{14,16},{16,18},{18... | collective-permute-start | bytes 497672 | tf_op jit(solution)/shard_map/ppermute | solution.py:53
  33.8 7.5 %collective-permute-start.3 = (bf16[72,1152]{1,0:T(8,128)(2,1)S(1)}, bf16[72,1152]{1,0:T(8,128)(2,1)S(1)}, u32[]{:S(2)}, u32[]{:S(2)}) collective-permute-start(bf16[72,1152]{1,0:T(8,128)(2,1)S(1)} %collective-permute-done.2), channel_id=1, source_target_pairs={{0,2},{2,4},{4,6},{6,8},{8,10},{10,12},{12,14},{14,16},{16,18},{18... | collective-permute-start | bytes 497672 | tf_op jit(solution)/shard_map/ppermute | solution.py:53
  41.3 10.0 %collective-permute-start.4 = (bf16[72,1152]{1,0:T(8,128)(2,1)S(1)}, bf16[72,1152]{1,0:T(8,128)(2,1)S(1)}, u32[]{:S(2)}, u32[]{:S(2)}) collective-permute-start(bf16[72,1152]{1,0:T(8,128)(2,1)S(1)} %collective-permute-done.3), channel_id=1, source_target_pairs={{0,2},{2,4},{4,6},{6,8},{8,10},{10,12},{12,14},{14,16},{16,18},{18... | collective-permute-start | bytes 497672 | tf_op jit(solution)/shard_map/ppermute | solution.py:53
  51.3 8.2 %collective-permute-start.5 = (bf16[72,1152]{1,0:T(8,128)(2,1)S(1)}, bf16[72,1152]{1,0:T(8,128)(2,1)S(1)}, u32[]{:S(2)}, u32[]{:S(2)}) collective-permute-start(bf16[72,1152]{1,0:T(8,128)(2,1)S(1)} %collective-permute-done.4), channel_id=1, source_target_pairs={{0,2},{2,4},{4,6},{6,8},{8,10},{10,12},{12,14},{14,16},{16,18},{18... | collective-permute-start | bytes 497672 | tf_op jit(solution)/shard_map/ppermute | solution.py:53
  59.5 7.5 %collective-permute-start.6 = (bf16[72,1152]{1,0:T(8,128)(2,1)S(1)}, bf16[72,1152]{1,0:T(8,128)(2,1)S(1)}, u32[]{:S(2)}, u32[]{:S(2)}) collective-permute-start(bf16[72,1152]{1,0:T(8,128)(2,1)S(1)} %collective-permute-done.5), channel_id=1, source_target_pairs={{0,2},{2,4},{4,6},{6,8},{8,10},{10,12},{12,14},{14,16},{16,18},{18... | collective-permute-start | bytes 497672 | tf_op jit(solution)/shard_map/ppermute | solution.py:53
  66.9 9.1 %collective-permute-start.7 = (bf16[72,1152]{1,0:T(8,128)(2,1)S(1)}, bf16[72,1152]{1,0:T(8,128)(2,1)S(1)}, u32[]{:S(2)}, u32[]{:S(2)}) collective-permute-start(bf16[72,1152]{1,0:T(8,128)(2,1)S(1)} %collective-permute-done.6), channel_id=1, source_target_pairs={{0,2},{2,4},{4,6},{6,8},{8,10},{10,12},{12,14},{14,16},{16,18},{18... | collective-permute-start | bytes 497672 | tf_op jit(solution)/shard_map/ppermute | solution.py:53
  76.0 7.8 %collective-permute-start.8 = (bf16[72,1152]{1,0:T(8,128)(2,1)S(1)}, bf16[72,1152]{1,0:T(8,128)(2,1)S(1)}, u32[]{:S(2)}, u32[]{:S(2)}) collective-permute-start(bf16[72,1152]{1,0:T(8,128)(2,1)S(1)} %collective-permute-done.7), channel_id=1, source_target_pairs={{0,2},{2,4},{4,6},{6,8},{8,10},{10,12},{12,14},{14,16},{16,18},{18... | collective-permute-start | bytes 497672 | tf_op jit(solution)/shard_map/ppermute | solution.py:53
  83.8 7.6 %collective-permute-start.9 = (bf16[72,1152]{1,0:T(8,128)(2,1)S(1)}, bf16[72,1152]{1,0:T(8,128)(2,1)S(1)}, u32[]{:S(2)}, u32[]{:S(2)}) collective-permute-start(bf16[72,1152]{1,0:T(8,128)(2,1)S(1)} %collective-permute-done.8), channel_id=1, source_target_pairs={{0,2},{2,4},{4,6},{6,8},{8,10},{10,12},{12,14},{14,16},{16,18},{18... | collective-permute-start | bytes 497672 | tf_op jit(solution)/shard_map/ppermute | solution.py:53
  91.4 8.7 %collective-permute-start.10 = (bf16[72,1152]{1,0:T(8,128)(2,1)S(1)}, bf16[72,1152]{1,0:T(8,128)(2,1)S(1)}, u32[]{:S(2)}, u32[]{:S(2)}) collective-permute-start(bf16[72,1152]{1,0:T(8,128)(2,1)S(1)} %collective-permute-done.9), channel_id=1, source_target_pairs={{0,2},{2,4},{4,6},{6,8},{8,10},{10,12},{12,14},{14,16},{16,18},{18... | collective-permute-start | bytes 497672 | tf_op jit(solution)/shard_map/ppermute | solution.py:53
  100.1 7.7 %collective-permute-start.11 = (bf16[72,1152]{1,0:T(8,128)(2,1)S(1)}, bf16[72,1152]{1,0:T(8,128)(2,1)S(1)}, u32[]{:S(2)}, u32[]{:S(2)}) collective-permute-start(bf16[72,1152]{1,0:T(8,128)(2,1)S(1)} %collective-permute-done.10), channel_id=1, source_target_pairs={{0,2},{2,4},{4,6},{6,8},{8,10},{10,12},{12,14},{14,16},{16,18},{18... | collective-permute-start | bytes 497672 | tf_op jit(solution)/shard_map/ppermute | solution.py:53
  107.9 7.5 %collective-permute-start.12 = (bf16[72,1152]{1,0:T(8,128)(2,1)S(1)}, bf16[72,1152]{1,0:T(8,128)(2,1)S(1)}, u32[]{:S(2)}, u32[]{:S(2)}) collective-permute-start(bf16[72,1152]{1,0:T(8,128)(2,1)S(1)} %collective-permute-done.11), channel_id=1, source_target_pairs={{0,2},{2,4},{4,6},{6,8},{8,10},{10,12},{12,14},{14,16},{16,18},{18... | collective-permute-start | bytes 497672 | tf_op jit(solution)/shard_map/ppermute | solution.py:53
  115.3 7.5 %collective-permute-start.13 = (bf16[72,1152]{1,0:T(8,128)(2,1)S(1)}, bf16[72,1152]{1,0:T(8,128)(2,1)S(1)}, u32[]{:S(2)}, u32[]{:S(2)}) collective-permute-start(bf16[72,1152]{1,0:T(8,128)(2,1)S(1)} %collective-permute-done.12), channel_id=1, source_target_pairs={{0,2},{2,4},{4,6},{6,8},{8,10},{10,12},{12,14},{14,16},{16,18},{18... | collective-permute-start | bytes 497672 | tf_op jit(solution)/shard_map/ppermute | solution.py:53
  122.8 7.5 %collective-permute-start.14 = (bf16[72,1152]{1,0:T(8,128)(2,1)S(1)}, bf16[72,1152]{1,0:T(8,128)(2,1)S(1)}, u32[]{:S(2)}, u32[]{:S(2)}) collective-permute-start(bf16[72,1152]{1,0:T(8,128)(2,1)S(1)} %collective-permute-done.13), channel_id=1, source_target_pairs={{0,2},{2,4},{4,6},{6,8},{8,10},{10,12},{12,14},{14,16},{16,18},{18... | collective-permute-start | bytes 497672 | tf_op jit(solution)/shard_map/ppermute | solution.py:53
  122.8 233.4 %reduce-scatter.4.cloned.1.call-start = ((), (), s32[]{:S(2)}) async-start(), calls=%async_computation.4 | async-start | bytes 11280384
  122.9 8.2 %copy-start.5 = (bf16[8,16,1152]{2,1,0:T(8,128)(2,1)S(1)}, bf16[8,16,1152]{2,1,0:T(8,128)(2,1)}, u32[]{:S(2)}) copy-start(bf16[8,16,1152]{2,1,0:T(8,128)(2,1)} %param.7) | copy-start | bytes 884740
  180.6 4.0 copy-start.7
  236.5 3.8 copy-start.2
  (3 other events, 10.2 us)
Sparse Core Ops, SparseCore 0:
  10.1 47.4 all-gather.7
  59.8 46.3 all-gather.3
  122.9 44.3 all-gather.5
  236.6 119.5 reduce-scatter.3
